TPU v7x, 256 devices: a whole 4x4x8 slice. The times are simulated.
256 devices in a mesh: ka: 8 (over x, core), gy: 8 (over z), gz: 4 (over y).
Axes of the slice: x: 4, y: 4, z: 8, core: 2. Of those that a mesh axis runs over, the one named last changes fastest.
Arguments:
- loads: float32 [128, 3, 256, 512], P('ka', None, 'gy', 'gz'), may hold values from -0.5 to 0.5
- sleeper_pos: int32 [128], P('ka'), may hold values from 0 to 127
- material: int32 [256, 512], P('gy', 'gz'), may hold values from 0 to 7, as said below
- material_table: float32 [8, 8], replicated, may hold values from -1 to 3, as said below
Outputs:
- adjoint_field: float32 [128, 2, 3, 256, 512], P('ka', None, None, 'gy', 'gz')
Inputs may be any that keep to these rules, and one draw needn't show every extreme that they name: layered: the material index never falls with depth in a column, layer boundaries vary from column to column, and every material occurs. `material_table`: shifts and damping positive, each material's coupling matrix diagonally dominant with a positive diagonal.
All inputs are finite; a program needn't handle non-finite values.
Results may differ from a plain program's by a relative error of at most 0.0002.
Values sent between devices are 32-bit elements; how exact they have to be, the bound alone decides.
A program may use at most 128 MiB of HBM per device.

v0:
```python
import math

import jax
import jax.numpy as jnp
from jax import lax
from jax.experimental import pallas as pl
from jax.experimental.pallas import tpu as pltpu
from jax.sharding import PartitionSpec as P

KW = 128
NMAT = 8
KA, GY, GZ = 8, 8, 4
LANES = 128
ROWS = 32
PART = ROWS // KA
STEPS = 7
MESH = pl.DeviceIdType.MESH
f32 = jnp.float32

LEAD = 3
ORDER = [(0, e) for e in range(LEAD)]
for e in range(STEPS):
    ORDER.append((1, e))
    if e + LEAD < STEPS:
        ORDER.append((0, e + LEAD))


def sine(angle):
    square = angle * angle
    value = jnp.full_like(angle, 1.0 / math.factorial(13))
    for degree in (11, 9, 7, 5, 3, 1):
        sign = -1.0 if (degree // 2) % 2 else 1.0
        value = value * square + sign / math.factorial(degree)
    return value * angle


def kernel(
    loads, pos, material, table, out,
    s1, r1, s2, wm, field, edge_out, edge_in, cells, coupling, per_k,
    p1_send, p1_recv, p2_send, p2_recv, halo_send, halo_recv,
):
    ka, gy, gz = lax.axis_index("ka"), lax.axis_index("gy"), lax.axis_index("gz")
    shape = (8, LANES)
    sub = lax.broadcasted_iota(jnp.int32, shape, 0)
    lane = lax.broadcasted_iota(jnp.int32, shape, 1)

    barrier = pltpu.get_barrier_semaphore()
    for o in range(1, KA):
        pl.semaphore_signal(
            barrier, inc=1, device_id={"ka": (ka + o) % KA}, device_id_type=MESH
        )
    for axis, at, size in (("gy", gy, GY), ("gz", gz, GZ)):
        for o in (1, size - 1):
            pl.semaphore_signal(
                barrier, inc=1, device_id={axis: (at + o) % size}, device_id_type=MESH
            )

    halves = []
    for h in range(2):
        position = jnp.zeros(shape, jnp.int32)
        for s in range(8):
            position = jnp.where(sub == s, pos[h * 8 + s], position)
        halves.append(position.astype(f32))

    def stage(o, carry):
        first = ((ka + o) % KA) * PART
        for h in range(2):
            s1[o, 0, h * 8 : h * 8 + 8, :] = halves[h]
            for yy in range(PART):
                for comp in range(3):
                    start = h * 8 * 96 + comp * ROWS + first + yy
                    s1[o, 1 + yy * 3 + comp, h * 8 : h * 8 + 8, :] = loads[
                        pl.ds(start, 8, stride=96), :
                    ]
        return carry

    lax.fori_loop(0, KA, stage, 0)
    zero = jnp.zeros(shape, f32)

    def clear_rows(row):
        for e in range(STEPS):
            for g in range(2):
                for c in range(6):
                    field[e, g, row, c] = zero

    def clear_columns(side):
        for e in range(STEPS):
            for g in range(2):
                for c in range(3):
                    edge_in[e, g, side, c] = zero

    pl.when(gy == 0)(lambda: clear_rows(0))
    pl.when(gy == GY - 1)(lambda: clear_rows(ROWS + 1))
    pl.when(gz == 0)(lambda: clear_columns(0))
    pl.when(gz == GZ - 1)(lambda: clear_columns(1))

    pl.semaphore_wait(barrier, KA - 1 + 4)

    def copy1(o):
        return pltpu.make_async_remote_copy(
            src_ref=s1.at[o],
            dst_ref=r1.at[ka],
            send_sem=p1_send.at[o],
            recv_sem=p1_recv.at[o],
            device_id={"ka": (ka + o) % KA},
            device_id_type=MESH,
        )

    def arrival1(o):
        return pltpu.make_async_remote_copy(
            src_ref=s1.at[o],
            dst_ref=r1.at[(ka + KA - o) % KA],
            send_sem=p1_send.at[o],
            recv_sem=p1_recv.at[o],
            device_id={"ka": (ka + o) % KA},
            device_id_type=MESH,
        )

    for o in (4, 3, 5, 2, 6, 1, 7):
        copy1(o).start()
    r1[ka] = s1[0]

    def gather_cells(t, carry):
        rows = pl.ds(pl.multiple_of(t * 8, 8), 8)
        index = material[rows, :]
        for f in range(8):
            value = jnp.zeros(shape, f32)
            for m in range(NMAT):
                value = jnp.where(index == m, table[m, f], value)
            cells[f, rows, :] = value
        return carry

    lax.fori_loop(0, ROWS // 8, gather_cells, 0)

    squares, centers = [], []
    for g in range(2):
        k = ka * 16 + g * 8 + sub
        half_turn = jnp.minimum(k, KW - k).astype(f32) * (math.pi / KW)
        root = 2.0 * sine(half_turn)
        q = root * root
        low, high = None, None
        for m in range(NMAT):
            entry = [jnp.full(shape, table[m, f], f32) for f in range(7)]
            off = [jnp.abs(entry[f]) for f in (4, 5, 6)]
            sums = (off[0] + off[1], off[0] + off[2], off[1] + off[2])
            lo = [entry[1 + c] - sums[c] for c in range(3)]
            hi = [entry[1 + c] + sums[c] for c in range(3)]
            lo = entry[0] + jnp.minimum(jnp.minimum(lo[0], lo[1]), lo[2]) * q
            hi = entry[0] + jnp.maximum(jnp.maximum(hi[0], hi[1]), hi[2]) * q
            low = lo if low is None else jnp.minimum(low, lo)
            high = hi if high is None else jnp.maximum(high, hi)
        high = 8.0 + high
        center = 0.5 * (high + low)
        width = 0.5 * (high - low)
        ratio = center / width
        weight = 1.0 / ratio
        d = [1.0 / center]
        r = [jnp.ones(shape, f32)]
        u = list(d)
        for _ in range(3):
            r = r + [zero]
            lowered = [center * d[j] if j < len(d) else zero for j in range(len(r))]
            raised = [zero] + d
            r = [r[j] - lowered[j] + raised[j] for j in range(len(r))]
            new_weight = 1.0 / (2.0 * ratio - weight)
            d = [
                (new_weight * weight) * (d[j] if j < len(d) else zero)
                + (2.0 * new_weight / width) * r[j]
                for j in range(len(r))
            ]
            u = [(u[j] if j < len(u) else zero) + d[j] for j in range(len(d))]
            weight = new_weight
        for j in range(4):
            per_k[g, j] = u[j]
        squares.append(q)
        centers.append(center)

    def prepare_coupling(y, carry):
        row = [cells[f, pl.ds(y, 1), :] for f in range(8)]
        for g in range(2):
            q = squares[g]
            base = centers[g] - 4.0 - row[0]
            for c in range(3):
                coupling[g, y, c] = base - q * row[1 + c]
                coupling[g, y, 3 + c] = -(q * row[4 + c])
            coupling[g, y, 6] = q * row[7]
        return carry

    lax.fori_loop(0, ROWS, prepare_coupling, 0)

    for o in range(1, KA):
        arrival1(o).wait_recv()
    positions = jnp.concatenate([r1[i, 0] for i in range(KA)], axis=0).T
    positions = jnp.concatenate([positions, positions], axis=0).astype(jnp.int32)
    wide = (256, LANES)
    row_no = lax.broadcasted_iota(jnp.int32, wide, 0)
    k_of = (row_no // 16) * 8 + row_no % 8
    imaginary = (row_no // 8) % 2
    turn = (k_of * positions + 32 * imaginary) & (KW - 1)
    away = jnp.abs(turn - KW // 2) - KW // 4
    weights = sine(away.astype(f32) * (2.0 * math.pi / KW))
    w_hi = weights.astype(jnp.bfloat16)
    w_lo = (weights - w_hi.astype(f32)).astype(jnp.bfloat16)
    wm[0:256, 0:128] = w_hi
    wm[0:256, 128:256] = w_hi
    wm[256:512, 0:128] = w_lo
    wm[256:512, 128:256] = jnp.zeros((256, 128), jnp.bfloat16)

    def transform(yy, carry):
        for comp in range(3):
            row = 1 + yy * 3 + comp
            values = jnp.concatenate([r1[i, row] for i in range(KA)], axis=0)
            v_hi = values.astype(jnp.bfloat16)
            v_lo = (values - v_hi.astype(f32)).astype(jnp.bfloat16)
            product = jnp.dot(
                wm[...], jnp.concatenate([v_hi, v_lo], axis=0), preferred_element_type=f32
            )
            product = product[0:256] + product[256:512]
            for d in range(KA):
                for g in range(2):
                    for ri in range(2):
                        at = ((d * 2 + g) * 2 + ri) * 8
                        s2[g, d, yy, ri * 3 + comp] = product[at : at + 8]
        return carry

    lax.fori_loop(0, PART, transform, 0)

    def copy2(g, o):
        return pltpu.make_async_remote_copy(
            src_ref=s2.at[g, (ka + o) % KA],
            dst_ref=field.at[0, g, pl.ds(1 + PART * ka, PART)],
            send_sem=p2_send.at[g, o],
            recv_sem=p2_recv.at[g, o],
            device_id={"ka": (ka + o) % KA},
            device_id_type=MESH,
        )

    def arrival2(g, o):
        return pltpu.make_async_remote_copy(
            src_ref=s2.at[g, (ka + o) % KA],
            dst_ref=field.at[0, g, pl.ds(1 + PART * ((ka + KA - o) % KA), PART)],
            send_sem=p2_send.at[g, o],
            recv_sem=p2_recv.at[g, o],
            device_id={"ka": (ka + o) % KA},
            device_id_type=MESH,
        )

    far_first = (4, 3, 5, 2, 6, 1, 7)
    for o in far_first:
        copy2(0, o).start()
    for g in range(2):
        field[0, g, pl.ds(1 + PART * ka, PART)] = s2[g, ka]
    for o in far_first:
        copy2(0, o).wait_send()
    for o in far_first:
        copy2(1, o).start()

    def row_copy(e, g, side):
        step = GY - 1 if side == 0 else 1
        return pltpu.make_async_remote_copy(
            src_ref=field.at[e, g, 1 if side == 0 else ROWS],
            dst_ref=field.at[e, g, ROWS + 1 if side == 0 else 0],
            send_sem=halo_send.at[e, g, side],
            recv_sem=halo_recv.at[e, g, side],
            device_id={"gy": (gy + step) % GY},
            device_id_type=MESH,
        )

    def row_arrival(e, g, side):
        step = GY - 1 if side == 0 else 1
        return pltpu.make_async_remote_copy(
            src_ref=field.at[e, g, 1 if side == 0 else ROWS],
            dst_ref=field.at[e, g, ROWS + 1 if side == 0 else 0],
            send_sem=halo_send.at[e, g, side],
            recv_sem=halo_recv.at[e, g, side],
            device_id={"gy": (gy + step) % GY},
            device_id_type=MESH,
        )

    def column_copy(e, g, side):
        step = GZ - 1 if side == 0 else 1
        return pltpu.make_async_remote_copy(
            src_ref=edge_out.at[e, g],
            dst_ref=edge_in.at[e, g, 1 - side],
            send_sem=halo_send.at[e, g, 2 + side],
            recv_sem=halo_recv.at[e, g, 2 + side],
            device_id={"gz": (gz + step) % GZ},
            device_id_type=MESH,
        )

    has_row = (gy > 0, gy < GY - 1)
    has_column = (gz > 0, gz < GZ - 1)

    def send_rows(e, g):
        for side in range(2):
            pl.when(has_row[side])(lambda: row_copy(e, g, side).start())

    def send_columns(e, g):
        for side in range(2):
            pl.when(has_column[side])(lambda: column_copy(e, g, side).start())

    def wait_halo(e, g):
        for side in range(2):
            pl.when(has_row[1 - side])(lambda: row_arrival(e, g, side).wait_recv())
            pl.when(has_column[1 - side])(lambda: column_copy(e, g, side).wait_recv())

    def finish(e, g):
        for side in range(2):
            pl.when(has_row[side])(lambda: row_copy(e, g, side).wait_send())
            pl.when(has_column[side])(lambda: column_copy(e, g, side).wait_send())

    owner = ((lane + 1) & (LANES - 1)) // 2
    even = (lane & 1) == 0
    first_lane = lane == 0
    last_lane = lane == LANES - 1

    def pack(packed, y, planes):
        real_at = owner == y
        imag_at = owner == y + ROWS
        return tuple(
            jnp.where(
                real_at,
                pltpu.roll(planes[c], 2 * y, 1),
                jnp.where(imag_at, pltpu.roll(planes[3 + c], 2 * y + 64, 1), packed[c]),
            )
            for c in range(3)
        )

    def receive(g):
        for o in far_first:
            arrival2(g, o).wait_recv()
        send_rows(0, g)

        def body(y, packed):
            return pack(packed, y, [field[0, g, y + 1, c] for c in range(6)])

        packed = lax.fori_loop(0, ROWS, body, (zero,) * 3, unroll=4)
        for c in range(3):
            edge_out[0, g, c] = packed[c]
        send_columns(0, g)

    def step(e, g):
        wait_halo(e, g)
        halo = []
        for c in range(3):
            halo.append(
                jnp.where(
                    even,
                    pltpu.roll(edge_in[e, g, 0, c], 1, 1),
                    pltpu.roll(edge_in[e, g, 1, c], LANES - 1, 1),
                )
            )
        scale = per_k[g, (2, 1, 0, 0, 2, 1, 0)[e]]
        outer = per_k[g, 3]

        def body(i, packed):
            y = (i * (ROWS - 1)) % ROWS
            here = [field[e, g, y + 1, c] for c in range(6)]
            k = [coupling[g, y, f] for f in range(7)]
            new = []
            for c in range(6):
                comp, other = c % 3, (c + 3) % 6
                side = pltpu.roll(
                    halo[comp], (2 * LANES - 2 * y) if c < 3 else (2 * LANES - 64 - 2 * y), 1
                )
                value = field[e, g, y, c] + field[e, g, y + 2, c]
                value += jnp.where(first_lane, side, pltpu.roll(here[c], 1, 1))
                value += jnp.where(last_lane, side, pltpu.roll(here[c], LANES - 1, 1))
                value += k[comp] * here[c]
                for j in range(3):
                    if j != comp:
                        value += k[2 + comp + j] * here[c - comp + j]
                if c < 3:
                    value += k[6] * here[other]
                else:
                    value -= k[6] * here[other]
                if e in (0, 4):
                    value = outer * value + scale * here[c]
                elif e in (1, 2):
                    value += scale * field[0, g, y + 1, c]
                elif e == 3:
                    value = field[0, g, y + 1, c] + (value - center_of(g) * here[c])
                else:
                    value += scale * field[4, g, y + 1, c]
                if e == 6:
                    value += field[3, g, y + 1, c]
                    out[pl.ds(g * 8 * 192 + c * ROWS + y, 8, stride=192), :] = value
                else:
                    field[e + 1, g, y + 1, c] = value
                new.append(value)
            return packed if e == 6 else pack(packed, y, new)

        if e == 6:
            lax.fori_loop(0, ROWS, body, (), unroll=2)
            return
        packed = lax.fori_loop(0, 2, body, (zero,) * 3)
        send_rows(e + 1, g)
        packed = lax.fori_loop(2, ROWS, body, packed, unroll=2)
        for c in range(3):
            edge_out[e + 1, g, c] = packed[c]
        send_columns(e + 1, g)

    def center_of(g):
        return centers[g]

    for g, e in ORDER:
        if e == 0:
            receive(g)
        step(e, g)

    for o in range(1, KA):
        copy1(o).wait_send()
        copy2(1, o).wait_send()
    for e in range(STEPS):
        for g in range(2):
            finish(e, g)


def local(loads, sleeper_pos, material, material_table):
    vmem = pl.BlockSpec(memory_space=pltpu.VMEM)
    smem = pl.BlockSpec(memory_space=pltpu.SMEM)
    dma = pltpu.SemaphoreType.DMA
    result = pl.pallas_call(
        kernel,
        out_shape=jax.ShapeDtypeStruct((16 * 6 * ROWS, LANES), f32),
        in_specs=[vmem, smem, vmem, smem],
        out_specs=vmem,
        scratch_shapes=[
            pltpu.VMEM((KA, 1 + 3 * PART, 16, LANES), f32),
            pltpu.VMEM((KA, 1 + 3 * PART, 16, LANES), f32),
            pltpu.VMEM((2, KA, PART, 6, 8, LANES), f32),
            pltpu.VMEM((512, 256), jnp.bfloat16),
            pltpu.VMEM((STEPS, 2, ROWS + 2, 6, 8, LANES), f32),
            pltpu.VMEM((STEPS, 2, 3, 8, LANES), f32),
            pltpu.VMEM((STEPS, 2, 2, 3, 8, LANES), f32),
            pltpu.VMEM((8, ROWS, LANES), f32),
            pltpu.VMEM((2, ROWS, 7, 8, LANES), f32),
            pltpu.VMEM((2, 4, 8, LANES), f32),
            dma((KA,)),
            dma((KA,)),
            dma((2, KA)),
            dma((2, KA)),
            dma((STEPS, 2, 4)),
            dma((STEPS, 2, 4)),
        ],
        compiler_params=pltpu.CompilerParams(
            collective_id=0, has_side_effects=True, vmem_limit_bytes=40 * 2**20
        ),
        name="adjoint",
    )(loads.reshape(16 * 3 * ROWS, LANES), sleeper_pos, material, material_table)
    return result.reshape(16, 2, 3, ROWS, LANES)


def solution(mesh):
    return jax.shard_map(
        local,
        mesh=mesh,
        in_specs=(P("ka", None, "gy", "gz"), P("ka"), P("gy", "gz"), P()),
        out_specs=P("ka", None, None, "gy", "gz"),
        check_vma=False,
    )
```

profile of v0, /device:TPU:8, one launch (start us, length us, event | category | flops | bytes accessed | tf_op | source)
XLA Modules:
  0.0 111.4 jit_solution(208755302921080447)
XLA Ops:
  0.0 0.0 copy-start
  0.0 1.1 %copy-done = f32[16,3,32,128]{3,2,1,0:T(8,128)S(1)} copy-done((f32[16,3,32,128]{3,2,1,0:T(8,128)S(1)}, f32[16,3,32,128]{3,2,1,0:T(8,128)}, u32[]{:S(2)}) %copy-start) | copy-done | bytes 786456
  1.1 0.0 copy-start.1
  1.1 0.7 copy-done.1
  1.9 0.0 copy-start.2
  1.9 0.7 copy-done.2
  2.5 0.0 copy-start.3
  2.5 0.7 copy-done.3
  3.2 107.0 %adjoint.1 = f32[3072,128]{1,0:T(8,128)S(1)} custom-call(f32[1536,128]{1,0:T(8,128)S(1)} %bitcast.3, s32[16]{0:T(128)S(1)} %copy-done.3, s32[32,128]{1,0:T(8,128)S(1)} %copy-done.1, f32[8,8]{1,0:T(8,128)S(1)} %copy-done.2), custom_call_target="tpu_custom_call" | custom-call | tf_op jit(solution)/shard_map/adjoint/pallas_call | solution.py:423
  110.2 1.1 %copy.6 = f32[16,2,3,32,128]{4,3,2,1,0:T(8,128)} copy(f32[16,2,3,32,128]{4,3,2,1,0:T(8,128)S(1)} %bitcast.2) | data formatting | bytes 3145728
Async XLA Ops:
  0.0 1.1 %copy-start = (f32[16,3,32,128]{3,2,1,0:T(8,128)S(1)}, f32[16,3,32,128]{3,2,1,0:T(8,128)}, u32[]{:S(2)}) copy-start(f32[16,3,32,128]{3,2,1,0:T(8,128)} %param.4) | copy-start | bytes 2359300
  1.1 0.7 copy-start.1
  1.9 0.7 copy-start.2
  2.5 0.7 copy-start.3
where the time goes:
time: 112 us; the launch traced here: 111 us
  Pallas kernels  107 us (96%)
  local copies, waits for them, and re-layouts  4.34 us (4%)
    pallas_call x1, Pallas kernels, local(): pl.pallas_call(kernel, out_shape=jax.ShapeDtypeStruct((16 * 6 * ROWS, LAN...  107 us
    unnamed x9, local copies, waits for them, and re-layouts  4.34 us

commit v1 on v0

v1 whole, which is shorter than its diff:
```python
import math

import jax
import jax.numpy as jnp
from jax import lax
from jax.experimental import pallas as pl
from jax.experimental.pallas import tpu as pltpu
from jax.sharding import PartitionSpec as P

KW = 128
NMAT = 8
KA, GY, GZ = 8, 8, 4
LANES = 128
ROWS = 32
PART = ROWS // KA
STEPS = 7
STRIP = 21
TOP, LEFT, RIGHT, ALL_ROWS = 8, 49, 59, 68
MESH = pl.DeviceIdType.MESH
f32 = jnp.float32


def sine(angle):
    square = angle * angle
    value = jnp.full_like(angle, 1.0 / math.factorial(13))
    for degree in (11, 9, 7, 5, 3, 1):
        sign = -1.0 if (degree // 2) % 2 else 1.0
        value = value * square + sign / math.factorial(degree)
    return value * angle


def kernel(
    loads, pos, material, table, out,
    s1, r1, s2, wm, f_b, f_a, f_c, f_u, f_r,
    strip_out, strip_in, corner_out, corner_in, mat, mat_in, mask, cells, coupling, per_k,
    p1_send, p1_recv, p2_send, p2_recv, halo_send, halo_recv, mat_send, mat_recv,
):
    ka, gy, gz = lax.axis_index("ka"), lax.axis_index("gy"), lax.axis_index("gz")
    shape = (8, LANES)
    sub = lax.broadcasted_iota(jnp.int32, shape, 0)
    lane = lax.broadcasted_iota(jnp.int32, shape, 1)

    barrier = pltpu.get_barrier_semaphore()
    for o in range(1, KA):
        pl.semaphore_signal(
            barrier, inc=1, device_id={"ka": (ka + o) % KA}, device_id_type=MESH
        )
    for dy in (-1, 0, 1):
        for dz in (-1, 0, 1):
            if dy or dz:
                pl.semaphore_signal(
                    barrier,
                    inc=1,
                    device_id={"gy": (gy + dy + GY) % GY, "gz": (gz + dz + GZ) % GZ},
                    device_id_type=MESH,
                )

    halves = []
    for h in range(2):
        position = jnp.zeros(shape, jnp.int32)
        for s in range(8):
            position = jnp.where(sub == s, pos[h * 8 + s], position)
        halves.append(position.astype(f32))

    def stage(o, carry):
        first = ((ka + o) % KA) * PART
        for h in range(2):
            s1[o, 0, h * 8 : h * 8 + 8, :] = halves[h]
            for yy in range(PART):
                for comp in range(3):
                    start = h * 8 * 96 + comp * ROWS + first + yy
                    s1[o, 1 + yy * 3 + comp, h * 8 : h * 8 + 8, :] = loads[
                        pl.ds(start, 8, stride=96), :
                    ]
        return carry

    lax.fori_loop(0, KA, stage, 0)
    zero = jnp.zeros(shape, f32)

    def clear_rows(first):
        def body(row, carry):
            for buffer in (f_b, f_a, f_c, f_u, f_r):
                for g in range(2):
                    for c in range(6):
                        buffer[g, row, c] = zero
            return carry

        lax.fori_loop(first, first + 8, body, 0)

    pl.when(gy == 0)(lambda: clear_rows(0))
    pl.when(gy == GY - 1)(lambda: clear_rows(TOP + ROWS))
    for t in range(ROWS // 8):
        mat[1 + t] = material[8 * t : 8 * t + 8, :]

    pl.semaphore_wait(barrier, KA - 1 + 8)

    exists = {-1: gy > 0, 1: gy < GY - 1}, {-1: gz > 0, 1: gz < GZ - 1}

    def send(src, dst, dy, dz, sends, recvs, at):
        copy = pltpu.make_async_remote_copy(
            src_ref=src,
            dst_ref=dst,
            send_sem=sends.at[at],
            recv_sem=recvs.at[at],
            device_id={"gy": (gy + dy + GY) % GY, "gz": (gz + dz + GZ) % GZ},
            device_id_type=MESH,
        )
        to, origin = True, True
        if dy:
            to, origin = exists[0][dy], exists[0][-dy]
        if dz:
            to = exists[1][dz] if to is True else jnp.logical_and(to, exists[1][dz])
            origin = exists[1][-dz] if origin is True else jnp.logical_and(origin, exists[1][-dz])
        return copy, to, origin

    def start(message):
        pl.when(message[1])(lambda: message[0].start())

    def finish(message):
        pl.when(message[1])(lambda: message[0].wait_send())

    def receive(message):
        pl.when(message[2])(lambda: message[0].wait_recv())

    mat_rows = (
        send(mat.at[1], mat.at[5], -1, 0, mat_send, mat_recv, 0),
        send(mat.at[4], mat.at[0], 1, 0, mat_send, mat_recv, 1),
    )
    mat_strips = (
        send(mat.at[6], mat_in.at[0], 0, 1, mat_send, mat_recv, 2),
        send(mat.at[7], mat_in.at[1], 0, -1, mat_send, mat_recv, 3),
    )
    for message in mat_rows:
        start(message)

    def copy1(o):
        return pltpu.make_async_remote_copy(
            src_ref=s1.at[o],
            dst_ref=r1.at[ka],
            send_sem=p1_send.at[o],
            recv_sem=p1_recv.at[o],
            device_id={"ka": (ka + o) % KA},
            device_id_type=MESH,
        )

    def arrival1(o):
        return pltpu.make_async_remote_copy(
            src_ref=s1.at[o],
            dst_ref=r1.at[(ka + KA - o) % KA],
            send_sem=p1_send.at[o],
            recv_sem=p1_recv.at[o],
            device_id={"ka": (ka + o) % KA},
            device_id_type=MESH,
        )

    for o in (4, 3, 5, 2, 6, 1, 7):
        copy1(o).start()
    r1[ka] = s1[0]

    block = lane // STRIP
    place = lane - block * STRIP
    for message in mat_rows:
        receive(message)
    for side in range(2):
        value = mat[5]
        value = pltpu.roll(value, (STRIP * 5 + 7 + 7 * side) % LANES, 1)
        for j in range(5):
            value = jnp.where(block == j, pltpu.roll(mat[j], STRIP * j + 7 + 7 * side, 1), value)
        mat[6 + side] = value
    for message in mat_strips:
        start(message)

    for side in range(2):
        row = gy * ROWS + 8 * block - 8
        column = gz * LANES + place + (LANES - 14 if side else -7)
        inside = jnp.logical_and(column >= 0, column < GZ * LANES)
        inside = jnp.logical_and(inside, block < 6)
        for i in range(8):
            valid = jnp.logical_and(row + i >= 0, row + i < GY * ROWS)
            if i == 0:
                valid = jnp.logical_and(valid, block > 0)
            if i == 7:
                valid = jnp.logical_and(valid, block < 5)
            mask[side, i] = jnp.where(jnp.logical_and(inside, valid), 1.0, 0.0)

    squares, centers = [], []
    for g in range(2):
        k = ka * 16 + g * 8 + sub
        half_turn = jnp.minimum(k, KW - k).astype(f32) * (math.pi / KW)
        root = 2.0 * sine(half_turn)
        q = root * root
        low, high = None, None
        for m in range(NMAT):
            entry = [jnp.full(shape, table[m, f], f32) for f in range(7)]
            off = [jnp.abs(entry[f]) for f in (4, 5, 6)]
            sums = (off[0] + off[1], off[0] + off[2], off[1] + off[2])
            lo = [entry[1 + c] - sums[c] for c in range(3)]
            hi = [entry[1 + c] + sums[c] for c in range(3)]
            lo = entry[0] + jnp.minimum(jnp.minimum(lo[0], lo[1]), lo[2]) * q
            hi = entry[0] + jnp.maximum(jnp.maximum(hi[0], hi[1]), hi[2]) * q
            low = lo if low is None else jnp.minimum(low, lo)
            high = hi if high is None else jnp.maximum(high, hi)
        high = 8.0 + high
        center = 0.5 * (high + low)
        width = 0.5 * (high - low)
        ratio = center / width
        weight = 1.0 / ratio
        d = [1.0 / center]
        r = [jnp.ones(shape, f32)]
        u = list(d)
        for _ in range(3):
            r = r + [zero]
            lowered = [center * d[j] if j < len(d) else zero for j in range(len(r))]
            raised = [zero] + d
            r = [r[j] - lowered[j] + raised[j] for j in range(len(r))]
            new_weight = 1.0 / (2.0 * ratio - weight)
            d = [
                (new_weight * weight) * (d[j] if j < len(d) else zero)
                + (2.0 * new_weight / width) * r[j]
                for j in range(len(r))
            ]
            u = [(u[j] if j < len(u) else zero) + d[j] for j in range(len(d))]
            weight = new_weight
        for j in range(4):
            per_k[g, j] = u[j]
        per_k[g, 4] = center
        squares.append(q)
        centers.append(center)

    for message in mat_strips:
        receive(message)
    foreign = (place < 7, place >= 14)
    mat_strip = [jnp.where(foreign[side], mat_in[side], mat[6 + side]) for side in range(2)]

    def gather_cells(t, carry):
        index = mat[t]
        rows = pl.ds(pl.multiple_of(t * 8, 8), 8)
        for f in range(8):
            value = jnp.zeros(shape, f32)
            for m in range(NMAT):
                value = jnp.where(index == m, table[m, f], value)
            cells[f, rows, :] = value
        return carry

    lax.fori_loop(0, 6, gather_cells, 0)
    for side in range(2):
        for f in range(8):
            value = jnp.zeros(shape, f32)
            for m in range(NMAT):
                value = jnp.where(mat_strip[side] == m, table[m, f], value)
            cells[f, 48 + 8 * side : 56 + 8 * side, :] = value

    def prepare_coupling(y, carry):
        row = [cells[f, pl.ds(y, 1), :] for f in range(8)]
        for g in range(2):
            q = squares[g]
            base = centers[g] - 4.0 - row[0]
            for c in range(3):
                coupling[g, y, c] = base - q * row[1 + c]
                coupling[g, y, 3 + c] = -(q * row[4 + c])
            coupling[g, y, 6] = q * row[7]
        return carry

    lax.fori_loop(0, 64, prepare_coupling, 0)

    for o in range(1, KA):
        arrival1(o).wait_recv()
    positions = jnp.concatenate([r1[i, 0] for i in range(KA)], axis=0).T
    positions = jnp.concatenate([positions, positions], axis=0).astype(jnp.int32)
    wide = (256, LANES)
    row_no = lax.broadcasted_iota(jnp.int32, wide, 0)
    k_of = (row_no // 16) * 8 + row_no % 8
    imaginary = (row_no // 8) % 2
    turn = (k_of * positions + 32 * imaginary) & (KW - 1)
    away = jnp.abs(turn - KW // 2) - KW // 4
    weights = sine(away.astype(f32) * (2.0 * math.pi / KW))
    w_hi = weights.astype(jnp.bfloat16)
    w_lo = (weights - w_hi.astype(f32)).astype(jnp.bfloat16)
    wm[0:256, 0:128] = w_hi
    wm[0:256, 128:256] = w_hi
    wm[256:512, 0:128] = w_lo
    wm[256:512, 128:256] = jnp.zeros((256, 128), jnp.bfloat16)

    def transform(yy, carry):
        for comp in range(3):
            row = 1 + yy * 3 + comp
            values = jnp.concatenate([r1[i, row] for i in range(KA)], axis=0)
            v_hi = values.astype(jnp.bfloat16)
            v_lo = (values - v_hi.astype(f32)).astype(jnp.bfloat16)
            product = jnp.dot(
                wm[...], jnp.concatenate([v_hi, v_lo], axis=0), preferred_element_type=f32
            )
            product = product[0:256] + product[256:512]
            for d in range(KA):
                for g in range(2):
                    for ri in range(2):
                        at = ((d * 2 + g) * 2 + ri) * 8
                        s2[g, d, yy, ri * 3 + comp] = product[at : at + 8]
        return carry

    lax.fori_loop(0, PART, transform, 0)

    def copy2(g, o):
        return pltpu.make_async_remote_copy(
            src_ref=s2.at[g, (ka + o) % KA],
            dst_ref=f_b.at[g, pl.ds(TOP + PART * ka, PART)],
            send_sem=p2_send.at[g, o],
            recv_sem=p2_recv.at[g, o],
            device_id={"ka": (ka + o) % KA},
            device_id_type=MESH,
        )

    def arrival2(g, o):
        return pltpu.make_async_remote_copy(
            src_ref=s2.at[g, (ka + o) % KA],
            dst_ref=f_b.at[g, pl.ds(TOP + PART * ((ka + KA - o) % KA), PART)],
            send_sem=p2_send.at[g, o],
            recv_sem=p2_recv.at[g, o],
            device_id={"ka": (ka + o) % KA},
            device_id_type=MESH,
        )

    far_first = (4, 3, 5, 2, 6, 1, 7)
    for o in far_first:
        copy2(0, o).start()
    for g in range(2):
        f_b[g, pl.ds(TOP + PART * ka, PART)] = s2[g, ka]
    for o in far_first:
        copy2(0, o).wait_send()
    for o in far_first:
        copy2(1, o).start()

    def messages(g):
        rows = (
            send(f_b.at[g, pl.ds(TOP, 7)], f_b.at[g, pl.ds(TOP + ROWS, 7)], -1, 0, halo_send, halo_recv, (g, 0)),
            send(f_b.at[g, pl.ds(TOP + ROWS - 7, 7)], f_b.at[g, pl.ds(1, 7)], 1, 0, halo_send, halo_recv, (g, 1)),
        )
        sides = (
            send(strip_out.at[g, 0], strip_in.at[g, 0], 0, 1, halo_send, halo_recv, (g, 2)),
            send(strip_out.at[g, 1], strip_in.at[g, 1], 0, -1, halo_send, halo_recv, (g, 3)),
        )
        corners = tuple(
            send(corner_out.at[g, n // 2], corner_in.at[g, n], dy, dz, halo_send, halo_recv, (g, 4 + n))
            for n, (dy, dz) in enumerate(((1, 1), (1, -1), (-1, 1), (-1, -1)))
        )
        return rows, sides + corners

    def exchange(g):
        for o in far_first:
            arrival2(g, o).wait_recv()
        rows, others = messages(g)
        for message in rows:
            start(message)

        def body(c, carry):
            near = [zero, zero]
            for i in range(8):
                values = [f_b[g, TOP + 8 * j + i, c] for j in range(4)]
                for side in range(2):
                    shift = 7 + 7 * side
                    strip = pltpu.roll(values[3], (STRIP * 4 + shift) % LANES, 1)
                    for j in (2, 1, 0):
                        strip = jnp.where(
                            block <= j + 1, pltpu.roll(values[j], STRIP * (j + 1) + shift, 1), strip
                        )
                    strip_out[g, side, i, c] = strip
                here = jnp.logical_and(lane >= 14 * i, lane < 14 * i + 14)
                near[0] = jnp.where(here, pltpu.roll(values[3], 14 * i + 7, 1), near[0])
                near[1] = jnp.where(here, pltpu.roll(values[0], 14 * i + 7, 1), near[1])
            corner_out[g, 0, c] = near[0]
            corner_out[g, 1, c] = near[1]
            return carry

        lax.fori_loop(0, 6, body, 0)
        for message in others:
            start(message)

    inner_block = jnp.logical_and(block >= 1, block <= 4)

    def wrap_strips(buffer, g, c):
        for first in (LEFT, RIGHT):
            buffer[g, first - 1, c] = pltpu.roll(buffer[g, first + 7, c], STRIP, 1)
            buffer[g, first + 8, c] = pltpu.roll(buffer[g, first, c], LANES - STRIP, 1)

    def assemble(g):
        masks = [[mask[side, i] > 0.5 for i in range(8)] for side in range(2)]

        def body(c, carry):
            for i in range(8):
                above, below = f_b[g, i, c], f_b[g, TOP + ROWS + i, c]
                for side in range(2):
                    shift = 7 + 7 * side
                    own = jnp.where(
                        block == 0,
                        pltpu.roll(above, shift, 1),
                        jnp.where(
                            block == 5,
                            pltpu.roll(below, (STRIP * 5 + shift) % LANES, 1),
                            strip_out[g, side, i, c],
                        ),
                    )
                    lower = 2 * LANES + 7 * side - 14 * i
                    other = jnp.where(
                        block == 0,
                        pltpu.roll(corner_in[g, side, c], lower % LANES, 1),
                        jnp.where(
                            block == 5,
                            pltpu.roll(corner_in[g, 2 + side, c], (lower + STRIP * 5) % LANES, 1),
                            strip_in[g, side, i, c],
                        ),
                    )
                    value = jnp.where(foreign[side], other, own)
                    f_b[g, (LEFT, RIGHT)[side] + i, c] = jnp.where(masks[side][i], value, 0.0)
            wrap_strips(f_b, g, c)
            return carry

        lax.fori_loop(0, 6, body, 0)

    source = (f_b, f_a, f_c, f_u, f_r, f_a, f_c)
    target = (f_a, f_c, f_u, f_r, f_a, f_c, f_a)

    def advance(e, g, at, cell, keep=None):
        src = source[e]
        here = [src[g, at, c] for c in range(6)]
        k = [coupling[g, cell, f] for f in range(7)]
        scale = per_k[g, (2, 1, 0, 4, 2, 1, 0)[e]]
        for c in range(6):
            comp, other = c % 3, (c + 3) % 6
            value = src[g, at - 1, c] + src[g, at + 1, c]
            value += pltpu.roll(here[c], 1, 1) + pltpu.roll(here[c], LANES - 1, 1)
            value += k[comp] * here[c]
            for j in range(3):
                if j != comp:
                    value += k[2 + comp + j] * here[c - comp + j]
            if c < 3:
                value += k[6] * here[other]
            else:
                value -= k[6] * here[other]
            if e in (0, 4):
                value = per_k[g, 3] * value + scale * here[c]
            elif e in (1, 2):
                value += scale * f_b[g, at, c]
            elif e == 3:
                value = f_b[g, at, c] + (value - scale * here[c])
            else:
                value += scale * f_r[g, at, c]
            if e == 6:
                value += f_u[g, at, c]
            if keep is not None:
                value *= keep
            target[e][g, at, c] = value

    def main_rows(e, g, first, count, unroll):
        def body(i, carry):
            advance(e, g, i + first, i + first)
            return carry

        lax.fori_loop(0, count, body, 0, unroll=unroll)

    def interior(g):
        for e in range(STEPS):
            main_rows(e, g, TOP + e + 1, 30 - 2 * e, (5, 4, 2, 4, 2, 5, 3)[e])

    def borders(g):
        for e in range(STEPS):
            beyond = 6 - e
            if beyond:
                pl.when(gy > 0)(lambda: main_rows(e, g, TOP - beyond, beyond, beyond))
                pl.when(gy < GY - 1)(lambda: main_rows(e, g, TOP + ROWS, beyond, beyond))
            main_rows(e, g, TOP, e + 1, e + 1)
            main_rows(e, g, TOP + ROWS - e - 1, e + 1, e + 1)

    def strips(g):
        for e in range(STEPS):

            def body(i, carry):
                advance(e, g, LEFT + i, 48 + i, mask[0, i])
                advance(e, g, RIGHT + i, 56 + i, mask[1, i])
                return carry

            lax.fori_loop(0, 8, body, 0, unroll=4)
            for c in range(6):
                wrap_strips(target[e], g, c)

    def deliver(g):
        edge = jnp.logical_or(lane < 7, lane >= LANES - 7)

        def body(i, carry):
            for c in range(6):
                joined = jnp.where(
                    place < 7, pltpu.roll(f_a[g, RIGHT + i, c], LANES - 7, 1), f_a[g, LEFT + i, c]
                )
                for j in range(4):
                    y = 8 * j + i
                    value = jnp.where(
                        edge,
                        pltpu.roll(joined, (2 * LANES - STRIP * (j + 1) - 7) % LANES, 1),
                        f_a[g, TOP + y, c],
                    )
                    out[pl.ds(g * 8 * 192 + c * ROWS + y, 8, stride=192), :] = value
            return carry

        lax.fori_loop(0, 8, body, 0)

    def await_halo(g):
        for group in messages(g):
            for message in group:
                receive(message)

    exchange(0)
    interior(0)
    await_halo(0)
    borders(0)
    exchange(1)
    assemble(0)
    strips(0)
    deliver(0)
    interior(1)
    await_halo(1)
    borders(1)
    assemble(1)
    strips(1)
    deliver(1)

    for o in range(1, KA):
        copy1(o).wait_send()
        copy2(1, o).wait_send()
    for message in mat_rows + mat_strips:
        finish(message)
    for g in range(2):
        for group in messages(g):
            for message in group:
                finish(message)


def local(loads, sleeper_pos, material, material_table):
    vmem = pl.BlockSpec(memory_space=pltpu.VMEM)
    smem = pl.BlockSpec(memory_space=pltpu.SMEM)
    dma = pltpu.SemaphoreType.DMA
    result = pl.pallas_call(
        kernel,
        out_shape=jax.ShapeDtypeStruct((16 * 6 * ROWS, LANES), f32),
        in_specs=[vmem, smem, vmem, smem],
        out_specs=vmem,
        scratch_shapes=[
            pltpu.VMEM((KA, 1 + 3 * PART, 16, LANES), f32),
            pltpu.VMEM((KA, 1 + 3 * PART, 16, LANES), f32),
            pltpu.VMEM((2, KA, PART, 6, 8, LANES), f32),
            pltpu.VMEM((512, 256), jnp.bfloat16),
            *[pltpu.VMEM((2, ALL_ROWS, 6, 8, LANES), f32)] * 5,
            pltpu.VMEM((2, 2, 8, 6, 8, LANES), f32),
            pltpu.VMEM((2, 2, 8, 6, 8, LANES), f32),
            pltpu.VMEM((2, 2, 6, 8, LANES), f32),
            pltpu.VMEM((2, 4, 6, 8, LANES), f32),
            pltpu.VMEM((8, 8, LANES), jnp.int32),
            pltpu.VMEM((2, 8, LANES), jnp.int32),
            pltpu.VMEM((2, 8, 8, LANES), f32),
            pltpu.VMEM((8, 64, LANES), f32),
            pltpu.VMEM((2, 64, 7, 8, LANES), f32),
            pltpu.VMEM((2, 5, 8, LANES), f32),
            dma((KA,)),
            dma((KA,)),
            dma((2, KA)),
            dma((2, KA)),
            dma((2, 8)),
            dma((2, 8)),
            dma((4,)),
            dma((4,)),
        ],
        compiler_params=pltpu.CompilerParams(
            collective_id=0, has_side_effects=True, vmem_limit_bytes=48 * 2**20
        ),
        name="adjoint",
    )(loads.reshape(16 * 3 * ROWS, LANES), sleeper_pos, material, material_table)
    return result.reshape(16, 2, 3, ROWS, LANES)


def solution(mesh):
    return jax.shard_map(
        local,
        mesh=mesh,
        in_specs=(P("ka", None, "gy", "gz"), P("ka"), P("gy", "gz"), P()),
        out_specs=P("ka", None, None, "gy", "gz"),
        check_vma=False,
    )
```

time: 112 us -> 68.3 us (0.61)
  the two profiles are of different devices: /device:TPU:8 before, /device:TPU:1 now
where the time goes in v1:
time: 68.3 us; the launch traced here: 68.1 us
  Pallas kernels  63.7 us (93%)
  local copies, waits for them, and re-layouts  4.34 us (6%)
    pallas_call x1, Pallas kernels, local(): pl.pallas_call(kernel, out_shape=jax.ShapeDtypeStruct((16 * 6 * ROWS, LAN...  63.7 us
    unnamed x9, local copies, waits for them, and re-layouts  4.34 us

profile of v1, /device:TPU:1, one launch (start us, length us, event | category | flops | bytes accessed | tf_op | source)
XLA Modules:
  0.0 68.1 jit_solution(2807579946120967679)
XLA Ops:
  0.0 0.0 copy-start
  0.0 1.1 %copy-done = f32[16,3,32,128]{3,2,1,0:T(8,128)S(1)} copy-done((f32[16,3,32,128]{3,2,1,0:T(8,128)S(1)}, f32[16,3,32,128]{3,2,1,0:T(8,128)}, u32[]{:S(2)}) %copy-start) | copy-done | bytes 786456
  1.1 0.0 copy-start.1
  1.1 0.7 %copy-done.1 = s32[32,128]{1,0:T(8,128)S(1)} copy-done((s32[32,128]{1,0:T(8,128)S(1)}, s32[32,128]{1,0:T(8,128)}, u32[]{:S(2)}) %copy-start.1) | copy-done | bytes 16408
  1.9 0.0 copy-start.2
  1.9 0.7 %copy-done.2 = f32[8,8]{1,0:T(8,128)S(1)} copy-done((f32[8,8]{1,0:T(8,128)S(1)}, f32[8,8]{1,0:T(8,128)}, u32[]{:S(2)}) %copy-start.2) | copy-done | bytes 280
  2.5 0.0 copy-start.3
  2.5 0.7 copy-done.3
  3.2 63.7 %adjoint.1 = f32[3072,128]{1,0:T(8,128)S(1)} custom-call(f32[1536,128]{1,0:T(8,128)S(1)} %bitcast.3, s32[16]{0:T(128)S(1)} %copy-done.3, s32[32,128]{1,0:T(8,128)S(1)} %copy-done.1, f32[8,8]{1,0:T(8,128)S(1)} %copy-done.2), custom_call_target="tpu_custom_call" | custom-call | tf_op jit(solution)/shard_map/adjoint/pallas_call | solution.py:540
  66.9 1.1 %copy.6 = f32[16,2,3,32,128]{4,3,2,1,0:T(8,128)} copy(f32[16,2,3,32,128]{4,3,2,1,0:T(8,128)S(1)} %bitcast.2) | data formatting | bytes 3145728
Async XLA Ops:
  0.0 1.1 %copy-start = (f32[16,3,32,128]{3,2,1,0:T(8,128)S(1)}, f32[16,3,32,128]{3,2,1,0:T(8,128)}, u32[]{:S(2)}) copy-start(f32[16,3,32,128]{3,2,1,0:T(8,128)} %param.4) | copy-start | bytes 2359300
  1.1 0.7 %copy-start.1 = (s32[32,128]{1,0:T(8,128)S(1)}, s32[32,128]{1,0:T(8,128)}, u32[]{:S(2)}) copy-start(s32[32,128]{1,0:T(8,128)} %material.1) | copy-start | bytes 49156
  1.9 0.7 %copy-start.2 = (f32[8,8]{1,0:T(8,128)S(1)}, f32[8,8]{1,0:T(8,128)}, u32[]{:S(2)}) copy-start(f32[8,8]{1,0:T(8,128)} %table.1) | copy-start | bytes 772
  2.5 0.7 copy-start.3

commit v2 on v1

--- a/solution.py
+++ b/solution.py
@@ -30,10 +30,10 @@
 
 
 def kernel(
-    loads, pos, material, table, out,
-    s1, r1, s2, wm, f_b, f_a, f_c, f_u, f_r,
+    loads_hbm, pos_hbm, material_hbm, table_hbm, out,
+    loads, pos, table, s1, r1, s2, wm, f_b, f_a, f_c, f_u, f_r, f_o,
     strip_out, strip_in, corner_out, corner_in, mat, mat_in, mask, cells, coupling, per_k,
-    p1_send, p1_recv, p2_send, p2_recv, halo_send, halo_recv, mat_send, mat_recv,
+    p1_send, p1_recv, p2_send, p2_recv, halo_send, halo_recv, mat_send, mat_recv, in_sem,
 ):
     ka, gy, gz = lax.axis_index("ka"), lax.axis_index("gy"), lax.axis_index("gz")
     shape = (8, LANES)
@@ -55,23 +55,36 @@
                     device_id_type=MESH,
                 )
 
-    halves = []
-    for h in range(2):
-        position = jnp.zeros(shape, jnp.int32)
-        for s in range(8):
-            position = jnp.where(sub == s, pos[h * 8 + s], position)
-        halves.append(position.astype(f32))
+    arguments = [
+        pltpu.make_async_copy(src, dst, in_sem.at[n])
+        for n, (src, dst) in enumerate(
+            (
+                (pos_hbm, pos),
+                (loads_hbm, loads),
+                (material_hbm, mat.at[pl.ds(1, ROWS // 8)]),
+                (table_hbm, table),
+            )
+        )
+    ]
+    for copy in arguments:
+        copy.start()
+    arguments[0].wait()
+
+    position = jnp.zeros(shape, jnp.int32)
+    for s in range(16):
+        position = jnp.where(lane == ka * 16 + s, pos[s], position)
+    position = position.astype(f32)
+    arguments[1].wait()
 
     def stage(o, carry):
         first = ((ka + o) % KA) * PART
+        s1[o, 0:8, :] = position
         for h in range(2):
-            s1[o, 0, h * 8 : h * 8 + 8, :] = halves[h]
             for yy in range(PART):
                 for comp in range(3):
                     start = h * 8 * 96 + comp * ROWS + first + yy
-                    s1[o, 1 + yy * 3 + comp, h * 8 : h * 8 + 8, :] = loads[
-                        pl.ds(start, 8, stride=96), :
-                    ]
+                    at = 8 + (yy * 3 + comp) * 16 + h * 8
+                    s1[o, at : at + 8, :] = loads[pl.ds(start, 8, stride=96), :]
         return carry
 
     lax.fori_loop(0, KA, stage, 0)
@@ -89,8 +102,8 @@
 
     pl.when(gy == 0)(lambda: clear_rows(0))
     pl.when(gy == GY - 1)(lambda: clear_rows(TOP + ROWS))
-    for t in range(ROWS // 8):
-        mat[1 + t] = material[8 * t : 8 * t + 8, :]
+    arguments[2].wait()
+    arguments[3].wait()
 
     pl.semaphore_wait(barrier, KA - 1 + 8)
 
@@ -265,8 +278,10 @@
 
     for o in range(1, KA):
         arrival1(o).wait_recv()
-    positions = jnp.concatenate([r1[i, 0] for i in range(KA)], axis=0).T
-    positions = jnp.concatenate([positions, positions], axis=0).astype(jnp.int32)
+    positions = r1[0, 0:1, :]
+    for i in range(1, KA):
+        positions += r1[i, 0:1, :]
+    positions = jnp.broadcast_to(positions, (256, LANES)).astype(jnp.int32)
     wide = (256, LANES)
     row_no = lax.broadcasted_iota(jnp.int32, wide, 0)
     k_of = (row_no // 16) * 8 + row_no % 8
@@ -283,8 +298,8 @@
 
     def transform(yy, carry):
         for comp in range(3):
-            row = 1 + yy * 3 + comp
-            values = jnp.concatenate([r1[i, row] for i in range(KA)], axis=0)
+            row = pl.ds(pl.multiple_of(8 + (yy * 3 + comp) * 16, 8), 16)
+            values = jnp.concatenate([r1[i, row, :] for i in range(KA)], axis=0)
             v_hi = values.astype(jnp.bfloat16)
             v_lo = (values - v_hi.astype(f32)).astype(jnp.bfloat16)
             product = jnp.dot(
@@ -327,7 +342,6 @@
         f_b[g, pl.ds(TOP + PART * ka, PART)] = s2[g, ka]
     for o in far_first:
         copy2(0, o).wait_send()
-    for o in far_first:
         copy2(1, o).start()
 
     def messages(g):
@@ -371,7 +385,7 @@
             corner_out[g, 1, c] = near[1]
             return carry
 
-        lax.fori_loop(0, 6, body, 0)
+        lax.fori_loop(0, 6, body, 0, unroll=2)
         for message in others:
             start(message)
 
@@ -411,13 +425,14 @@
                     )
                     value = jnp.where(foreign[side], other, own)
                     f_b[g, (LEFT, RIGHT)[side] + i, c] = jnp.where(masks[side][i], value, 0.0)
+            return carry
+
+        lax.fori_loop(0, 6, body, 0, unroll=2)
+        for c in range(6):
             wrap_strips(f_b, g, c)
-            return carry
-
-        lax.fori_loop(0, 6, body, 0)
 
     source = (f_b, f_a, f_c, f_u, f_r, f_a, f_c)
-    target = (f_a, f_c, f_u, f_r, f_a, f_c, f_a)
+    target = (f_a, f_c, f_u, f_r, f_a, f_c, f_o)
 
     def advance(e, g, at, cell, keep=None):
         src = source[e]
@@ -459,28 +474,26 @@
 
     def interior(g):
         for e in range(STEPS):
-            main_rows(e, g, TOP + e + 1, 30 - 2 * e, (5, 4, 2, 4, 2, 5, 3)[e])
-
-    def borders(g):
+            main_rows(e, g, TOP + e + 1, 30 - 2 * e, (15, 14, 13, 12, 11, 10, 9)[e])
+
+    def borders_and_strips(g):
+        above = jnp.where(gy > 0, 1.0, 0.0)
+        below = jnp.where(gy < GY - 1, 1.0, 0.0)
         for e in range(STEPS):
-            beyond = 6 - e
-            if beyond:
-                pl.when(gy > 0)(lambda: main_rows(e, g, TOP - beyond, beyond, beyond))
-                pl.when(gy < GY - 1)(lambda: main_rows(e, g, TOP + ROWS, beyond, beyond))
-            main_rows(e, g, TOP, e + 1, e + 1)
-            main_rows(e, g, TOP + ROWS - e - 1, e + 1, e + 1)
-
-    def strips(g):
-        for e in range(STEPS):
 
             def body(i, carry):
+                at = TOP - 6 + e + i
+                advance(e, g, at, at, jnp.where(i < 6 - e, above, 1.0))
+                at = TOP + ROWS - 2 - e + i
+                advance(e, g, at, at, jnp.where(i >= e + 2, below, 1.0))
                 advance(e, g, LEFT + i, 48 + i, mask[0, i])
                 advance(e, g, RIGHT + i, 56 + i, mask[1, i])
                 return carry
 
-            lax.fori_loop(0, 8, body, 0, unroll=4)
-            for c in range(6):
-                wrap_strips(target[e], g, c)
+            lax.fori_loop(0, 8, body, 0, unroll=8)
+            if e < STEPS - 1:
+                for c in range(6):
+                    wrap_strips(target[e], g, c)
 
     def deliver(g):
         edge = jnp.logical_or(lane < 7, lane >= LANES - 7)
@@ -488,19 +501,19 @@
         def body(i, carry):
             for c in range(6):
                 joined = jnp.where(
-                    place < 7, pltpu.roll(f_a[g, RIGHT + i, c], LANES - 7, 1), f_a[g, LEFT + i, c]
+                    place < 7, pltpu.roll(f_o[g, RIGHT + i, c], LANES - 7, 1), f_o[g, LEFT + i, c]
                 )
                 for j in range(4):
                     y = 8 * j + i
                     value = jnp.where(
                         edge,
                         pltpu.roll(joined, (2 * LANES - STRIP * (j + 1) - 7) % LANES, 1),
-                        f_a[g, TOP + y, c],
+                        f_o[g, TOP + y, c],
                     )
                     out[pl.ds(g * 8 * 192 + c * ROWS + y, 8, stride=192), :] = value
             return carry
 
-        lax.fori_loop(0, 8, body, 0)
+        lax.fori_loop(0, 8, body, 0, unroll=4)
 
     def await_halo(g):
         for group in messages(g):
@@ -510,16 +523,14 @@
     exchange(0)
     interior(0)
     await_halo(0)
-    borders(0)
+    assemble(0)
     exchange(1)
-    assemble(0)
-    strips(0)
+    borders_and_strips(0)
     deliver(0)
     interior(1)
     await_halo(1)
-    borders(1)
     assemble(1)
-    strips(1)
+    borders_and_strips(1)
     deliver(1)
 
     for o in range(1, KA):
@@ -535,19 +546,22 @@
 
 def local(loads, sleeper_pos, material, material_table):
     vmem = pl.BlockSpec(memory_space=pltpu.VMEM)
-    smem = pl.BlockSpec(memory_space=pltpu.SMEM)
+    hbm = pl.BlockSpec(memory_space=pltpu.HBM)
     dma = pltpu.SemaphoreType.DMA
     result = pl.pallas_call(
         kernel,
         out_shape=jax.ShapeDtypeStruct((16 * 6 * ROWS, LANES), f32),
-        in_specs=[vmem, smem, vmem, smem],
+        in_specs=[hbm] * 4,
         out_specs=vmem,
         scratch_shapes=[
-            pltpu.VMEM((KA, 1 + 3 * PART, 16, LANES), f32),
-            pltpu.VMEM((KA, 1 + 3 * PART, 16, LANES), f32),
+            pltpu.VMEM((16 * 3 * ROWS, LANES), f32),
+            pltpu.SMEM((16,), jnp.int32),
+            pltpu.SMEM((NMAT, 8), f32),
+            pltpu.VMEM((KA, 8 + 3 * PART * 16, LANES), f32),
+            pltpu.VMEM((KA, 8 + 3 * PART * 16, LANES), f32),
             pltpu.VMEM((2, KA, PART, 6, 8, LANES), f32),
             pltpu.VMEM((512, 256), jnp.bfloat16),
-            *[pltpu.VMEM((2, ALL_ROWS, 6, 8, LANES), f32)] * 5,
+            *[pltpu.VMEM((2, ALL_ROWS, 6, 8, LANES), f32)] * 6,
             pltpu.VMEM((2, 2, 8, 6, 8, LANES), f32),
             pltpu.VMEM((2, 2, 8, 6, 8, LANES), f32),
             pltpu.VMEM((2, 2, 6, 8, LANES), f32),
@@ -566,12 +580,13 @@
             dma((2, 8)),
             dma((4,)),
             dma((4,)),
+            dma((4,)),
         ],
         compiler_params=pltpu.CompilerParams(
             collective_id=0, has_side_effects=True, vmem_limit_bytes=48 * 2**20
         ),
         name="adjoint",
-    )(loads.reshape(16 * 3 * ROWS, LANES), sleeper_pos, material, material_table)
+    )(loads.reshape(16 * 3 * ROWS, LANES), sleeper_pos, material.reshape(ROWS // 8, 8, LANES), material_table)
     return result.reshape(16, 2, 3, ROWS, LANES)
 
 

time: 68.3 us -> 59.5 us (0.87)
  Pallas kernels: 63.7 us -> 55 us
    pallas_call x1, Pallas kernels: 63.7 us -> 55 us  [local(): pl.pallas_call(kernel, out_shape=jax.ShapeDtypeStruct((16 * 6 * ROWS, LAN...]
where the time goes in v2:
time: 59.5 us; the launch traced here: 59.3 us
  Pallas kernels  55 us (92%)
  local copies, waits for them, and re-layouts  4.34 us (7%)
    pallas_call x1, Pallas kernels, local(): pl.pallas_call(kernel, out_shape=jax.ShapeDtypeStruct((16 * 6 * ROWS, LAN...  55 us
    unnamed x9, local copies, waits for them, and re-layouts  4.34 us

profile of v2, /device:TPU:1, one launch (start us, length us, event | category | flops | bytes accessed | tf_op | source)
XLA Modules:
  0.0 59.3 jit_solution(17086261141900403566)
XLA Ops:
  0.0 0.0 copy-start
  0.0 1.1 %copy-done = f32[16,3,32,128]{3,2,1,0:T(8,128)S(1)} copy-done((f32[16,3,32,128]{3,2,1,0:T(8,128)S(1)}, f32[16,3,32,128]{3,2,1,0:T(8,128)}, u32[]{:S(2)}) %copy-start) | copy-done | bytes 786456
  1.1 0.0 copy-start.1
  1.1 0.7 %copy-done.1 = s32[32,128]{1,0:T(8,128)S(1)} copy-done((s32[32,128]{1,0:T(8,128)S(1)}, s32[32,128]{1,0:T(8,128)}, u32[]{:S(2)}) %copy-start.1) | copy-done | bytes 16408
  1.9 0.0 copy-start.2
  1.9 0.7 %copy-done.2 = f32[8,8]{1,0:T(8,128)S(1)} copy-done((f32[8,8]{1,0:T(8,128)S(1)}, f32[8,8]{1,0:T(8,128)}, u32[]{:S(2)}) %copy-start.2) | copy-done | bytes 280
  2.5 0.0 copy-start.3
  2.5 0.7 %copy-done.3 = s32[16]{0:T(128)S(1)} copy-done((s32[16]{0:T(128)S(1)}, s32[16]{0:T(128)}, u32[]{:S(2)}) %copy-start.3) | copy-done | bytes 88
  3.2 55.0 %adjoint.1 = f32[3072,128]{1,0:T(8,128)S(1)} custom-call(f32[1536,128]{1,0:T(8,128)S(1)} %bitcast.4, s32[16]{0:T(128)S(1)} %copy-done.3, s32[4,8,128]{2,1,0:T(8,128)S(1)} %bitcast.5, f32[8,8]{1,0:T(8,128)S(1)} %copy-done.2), custom_call_target="tpu_custom_call" | custom-call | tf_op jit(solution)/shard_map/adjoint/pallas_call | solution.py:551
  58.2 1.1 %copy.6 = f32[16,2,3,32,128]{4,3,2,1,0:T(8,128)} copy(f32[16,2,3,32,128]{4,3,2,1,0:T(8,128)S(1)} %bitcast.3) | data formatting | bytes 3145728
Async XLA Ops:
  0.0 1.1 %copy-start = (f32[16,3,32,128]{3,2,1,0:T(8,128)S(1)}, f32[16,3,32,128]{3,2,1,0:T(8,128)}, u32[]{:S(2)}) copy-start(f32[16,3,32,128]{3,2,1,0:T(8,128)} %param.4) | copy-start | bytes 2359300
  1.1 0.7 %copy-start.1 = (s32[32,128]{1,0:T(8,128)S(1)}, s32[32,128]{1,0:T(8,128)}, u32[]{:S(2)}) copy-start(s32[32,128]{1,0:T(8,128)} %param.6) | copy-start | bytes 49156
  1.9 0.7 %copy-start.2 = (f32[8,8]{1,0:T(8,128)S(1)}, f32[8,8]{1,0:T(8,128)}, u32[]{:S(2)}) copy-start(f32[8,8]{1,0:T(8,128)} %table_hbm.1) | copy-start | bytes 772
  2.5 0.7 %copy-start.3 = (s32[16]{0:T(128)S(1)}, s32[16]{0:T(128)}, u32[]{:S(2)}) copy-start(s32[16]{0:T(128)} %pos_hbm.1) | copy-start | bytes 196

commit v3 on v2

--- a/solution.py
+++ b/solution.py
@@ -146,28 +146,22 @@
     for message in mat_rows:
         start(message)
 
-    def copy1(o):
+    early, late = pl.ds(0, 8 + PART * 24), pl.ds(8 + PART * 24, PART * 24)
+
+    def copy1(part, o, source):
+        rows = late if part else early
         return pltpu.make_async_remote_copy(
-            src_ref=s1.at[o],
-            dst_ref=r1.at[ka],
-            send_sem=p1_send.at[o],
-            recv_sem=p1_recv.at[o],
+            src_ref=s1.at[o, rows],
+            dst_ref=r1.at[source, rows],
+            send_sem=p1_send.at[part, o],
+            recv_sem=p1_recv.at[part, o],
             device_id={"ka": (ka + o) % KA},
             device_id_type=MESH,
         )
 
-    def arrival1(o):
-        return pltpu.make_async_remote_copy(
-            src_ref=s1.at[o],
-            dst_ref=r1.at[(ka + KA - o) % KA],
-            send_sem=p1_send.at[o],
-            recv_sem=p1_recv.at[o],
-            device_id={"ka": (ka + o) % KA},
-            device_id_type=MESH,
-        )
-
-    for o in (4, 3, 5, 2, 6, 1, 7):
-        copy1(o).start()
+    far_first = (4, 3, 5, 2, 6, 1, 7)
+    for o in far_first:
+        copy1(0, o, ka).start()
     r1[ka] = s1[0]
 
     block = lane // STRIP
@@ -240,6 +234,10 @@
         squares.append(q)
         centers.append(center)
 
+    for o in far_first:
+        copy1(0, o, ka).wait_send()
+        copy1(1, o, ka).start()
+
     for message in mat_strips:
         receive(message)
     foreign = (place < 7, place >= 14)
@@ -277,7 +275,7 @@
     lax.fori_loop(0, 64, prepare_coupling, 0)
 
     for o in range(1, KA):
-        arrival1(o).wait_recv()
+        copy1(0, o, (ka + KA - o) % KA).wait_recv()
     positions = r1[0, 0:1, :]
     for i in range(1, KA):
         positions += r1[i, 0:1, :]
@@ -313,36 +311,35 @@
                         s2[g, d, yy, ri * 3 + comp] = product[at : at + 8]
         return carry
 
-    lax.fori_loop(0, PART, transform, 0)
-
-    def copy2(g, o):
+    first_row = (0, PART // 2, 0)
+    row_count = (PART // 2, PART // 2, PART)
+
+    def copy2(part, o, source):
+        g, first, count = part // 2, first_row[part], row_count[part]
         return pltpu.make_async_remote_copy(
-            src_ref=s2.at[g, (ka + o) % KA],
-            dst_ref=f_b.at[g, pl.ds(TOP + PART * ka, PART)],
-            send_sem=p2_send.at[g, o],
-            recv_sem=p2_recv.at[g, o],
+            src_ref=s2.at[g, (ka + o) % KA, pl.ds(first, count)],
+            dst_ref=f_b.at[g, pl.ds(TOP + PART * source + first, count)],
+            send_sem=p2_send.at[part, o],
+            recv_sem=p2_recv.at[part, o],
             device_id={"ka": (ka + o) % KA},
             device_id_type=MESH,
         )
 
-    def arrival2(g, o):
-        return pltpu.make_async_remote_copy(
-            src_ref=s2.at[g, (ka + o) % KA],
-            dst_ref=f_b.at[g, pl.ds(TOP + PART * ((ka + KA - o) % KA), PART)],
-            send_sem=p2_send.at[g, o],
-            recv_sem=p2_recv.at[g, o],
-            device_id={"ka": (ka + o) % KA},
-            device_id_type=MESH,
-        )
-
-    far_first = (4, 3, 5, 2, 6, 1, 7)
+    lax.fori_loop(0, PART // 2, transform, 0)
     for o in far_first:
-        copy2(0, o).start()
+        copy2(0, o, ka).start()
+    for o in range(1, KA):
+        copy1(1, o, (ka + KA - o) % KA).wait_recv()
+    lax.fori_loop(PART // 2, PART, transform, 0)
+    for o in far_first:
+        copy2(1, o, ka).start()
     for g in range(2):
         f_b[g, pl.ds(TOP + PART * ka, PART)] = s2[g, ka]
     for o in far_first:
-        copy2(0, o).wait_send()
-        copy2(1, o).start()
+        copy2(0, o, ka).wait_send()
+    for o in far_first:
+        copy2(1, o, ka).wait_send()
+        copy2(2, o, ka).start()
 
     def messages(g):
         rows = (
@@ -360,8 +357,9 @@
         return rows, sides + corners
 
     def exchange(g):
-        for o in far_first:
-            arrival2(g, o).wait_recv()
+        for part in (2,) if g else (0, 1):
+            for o in far_first:
+                copy2(part, o, (ka + KA - o) % KA).wait_recv()
         rows, others = messages(g)
         for message in rows:
             start(message)
@@ -534,8 +532,8 @@
     deliver(1)
 
     for o in range(1, KA):
-        copy1(o).wait_send()
-        copy2(1, o).wait_send()
+        copy1(1, o, ka).wait_send()
+        copy2(2, o, ka).wait_send()
     for message in mat_rows + mat_strips:
         finish(message)
     for g in range(2):
@@ -572,10 +570,10 @@
             pltpu.VMEM((8, 64, LANES), f32),
             pltpu.VMEM((2, 64, 7, 8, LANES), f32),
             pltpu.VMEM((2, 5, 8, LANES), f32),
-            dma((KA,)),
-            dma((KA,)),
             dma((2, KA)),
             dma((2, KA)),
+            dma((3, KA)),
+            dma((3, KA)),
             dma((2, 8)),
             dma((2, 8)),
             dma((4,)),

time: 59.5 us -> 56 us (0.941)
  Pallas kernels: 55 us -> 51.4 us
    pallas_call x1, Pallas kernels: 55 us -> 51.4 us  [local(): pl.pallas_call(kernel, out_shape=jax.ShapeDtypeStruct((16 * 6 * ROWS, LAN...]
where the time goes in v3:
time: 56 us; the launch traced here: 55.8 us
  Pallas kernels  51.4 us (92%)
  local copies, waits for them, and re-layouts  4.34 us (8%)
    pallas_call x1, Pallas kernels, local(): pl.pallas_call(kernel, out_shape=jax.ShapeDtypeStruct((16 * 6 * ROWS, LAN...  51.4 us
    unnamed x9, local copies, waits for them, and re-layouts  4.34 us

profile of v3, /device:TPU:1, one launch (start us, length us, event | category | flops | bytes accessed | tf_op | source)
XLA Modules:
  0.0 55.8 jit_solution(10229208366384657166)
XLA Ops:
  0.0 0.0 copy-start
  0.0 1.1 %copy-done = f32[16,3,32,128]{3,2,1,0:T(8,128)S(1)} copy-done((f32[16,3,32,128]{3,2,1,0:T(8,128)S(1)}, f32[16,3,32,128]{3,2,1,0:T(8,128)}, u32[]{:S(2)}) %copy-start) | copy-done | bytes 786456
  1.1 0.0 copy-start.1
  1.1 0.7 %copy-done.1 = s32[32,128]{1,0:T(8,128)S(1)} copy-done((s32[32,128]{1,0:T(8,128)S(1)}, s32[32,128]{1,0:T(8,128)}, u32[]{:S(2)}) %copy-start.1) | copy-done | bytes 16408
  1.9 0.0 copy-start.2
  1.9 0.7 %copy-done.2 = f32[8,8]{1,0:T(8,128)S(1)} copy-done((f32[8,8]{1,0:T(8,128)S(1)}, f32[8,8]{1,0:T(8,128)}, u32[]{:S(2)}) %copy-start.2) | copy-done | bytes 280
  2.5 0.0 copy-start.3
  2.5 0.7 %copy-done.3 = s32[16]{0:T(128)S(1)} copy-done((s32[16]{0:T(128)S(1)}, s32[16]{0:T(128)}, u32[]{:S(2)}) %copy-start.3) | copy-done | bytes 88
  3.2 51.4 %adjoint.1 = f32[3072,128]{1,0:T(8,128)S(1)} custom-call(f32[1536,128]{1,0:T(8,128)S(1)} %bitcast.4, s32[16]{0:T(128)S(1)} %copy-done.3, s32[4,8,128]{2,1,0:T(8,128)S(1)} %bitcast.5, f32[8,8]{1,0:T(8,128)S(1)} %copy-done.2), custom_call_target="tpu_custom_call" | custom-call | tf_op jit(solution)/shard_map/adjoint/pallas_call | solution.py:549
  54.6 1.1 %copy.6 = f32[16,2,3,32,128]{4,3,2,1,0:T(8,128)} copy(f32[16,2,3,32,128]{4,3,2,1,0:T(8,128)S(1)} %bitcast.3) | data formatting | bytes 3145728
Async XLA Ops:
  0.0 1.1 %copy-start = (f32[16,3,32,128]{3,2,1,0:T(8,128)S(1)}, f32[16,3,32,128]{3,2,1,0:T(8,128)}, u32[]{:S(2)}) copy-start(f32[16,3,32,128]{3,2,1,0:T(8,128)} %param.4) | copy-start | bytes 2359300
  1.1 0.7 %copy-start.1 = (s32[32,128]{1,0:T(8,128)S(1)}, s32[32,128]{1,0:T(8,128)}, u32[]{:S(2)}) copy-start(s32[32,128]{1,0:T(8,128)} %param.6) | copy-start | bytes 49156
  1.9 0.7 %copy-start.2 = (f32[8,8]{1,0:T(8,128)S(1)}, f32[8,8]{1,0:T(8,128)}, u32[]{:S(2)}) copy-start(f32[8,8]{1,0:T(8,128)} %table_hbm.1) | copy-start | bytes 772
  2.5 0.7 %copy-start.3 = (s32[16]{0:T(128)S(1)}, s32[16]{0:T(128)}, u32[]{:S(2)}) copy-start(s32[16]{0:T(128)} %pos_hbm.1) | copy-start | bytes 196

commit v4 on v3

--- a/solution.py
+++ b/solution.py
@@ -30,10 +30,10 @@
 
 
 def kernel(
-    loads_hbm, pos_hbm, material_hbm, table_hbm, out,
-    loads, pos, table, s1, r1, s2, wm, f_b, f_a, f_c, f_u, f_r, f_o,
+    loads_hbm, pos_hbm, material_hbm, table_hbm, out_hbm,
+    out, loads, pos, table, s1, r1, s2, wm, f_b, f_a, f_c, f_u, f_r, f_o,
     strip_out, strip_in, corner_out, corner_in, mat, mat_in, mask, cells, coupling, per_k,
-    p1_send, p1_recv, p2_send, p2_recv, halo_send, halo_recv, mat_send, mat_recv, in_sem,
+    p1_send, p1_recv, p2_send, p2_recv, halo_send, halo_recv, mat_send, mat_recv, in_sem, out_sem,
 ):
     ka, gy, gz = lax.axis_index("ka"), lax.axis_index("gy"), lax.axis_index("gz")
     shape = (8, LANES)
@@ -513,6 +513,10 @@
 
         lax.fori_loop(0, 8, body, 0, unroll=4)
 
+    def result(g):
+        rows = pl.ds(g * 8 * 192, 8 * 192)
+        return pltpu.make_async_copy(out.at[rows], out_hbm.at[rows], out_sem.at[g])
+
     def await_halo(g):
         for group in messages(g):
             for message in group:
@@ -525,15 +529,19 @@
     exchange(1)
     borders_and_strips(0)
     deliver(0)
+    result(0).start()
     interior(1)
     await_halo(1)
     assemble(1)
     borders_and_strips(1)
     deliver(1)
+    result(1).start()
 
     for o in range(1, KA):
         copy1(1, o, ka).wait_send()
         copy2(2, o, ka).wait_send()
+    result(0).wait()
+    result(1).wait()
     for message in mat_rows + mat_strips:
         finish(message)
     for g in range(2):
@@ -543,15 +551,15 @@
 
 
 def local(loads, sleeper_pos, material, material_table):
-    vmem = pl.BlockSpec(memory_space=pltpu.VMEM)
     hbm = pl.BlockSpec(memory_space=pltpu.HBM)
     dma = pltpu.SemaphoreType.DMA
     result = pl.pallas_call(
         kernel,
         out_shape=jax.ShapeDtypeStruct((16 * 6 * ROWS, LANES), f32),
         in_specs=[hbm] * 4,
-        out_specs=vmem,
+        out_specs=hbm,
         scratch_shapes=[
+            pltpu.VMEM((16 * 6 * ROWS, LANES), f32),
             pltpu.VMEM((16 * 3 * ROWS, LANES), f32),
             pltpu.SMEM((16,), jnp.int32),
             pltpu.SMEM((NMAT, 8), f32),
@@ -579,9 +587,10 @@
             dma((4,)),
             dma((4,)),
             dma((4,)),
+            dma((2,)),
         ],
         compiler_params=pltpu.CompilerParams(
-            collective_id=0, has_side_effects=True, vmem_limit_bytes=48 * 2**20
+            collective_id=0, has_side_effects=True, vmem_limit_bytes=60 * 2**20
         ),
         name="adjoint",
     )(loads.reshape(16 * 3 * ROWS, LANES), sleeper_pos, material.reshape(ROWS // 8, 8, LANES), material_table)

time: 56 us -> 55.2 us (0.986)
  local copies, waits for them, and re-layouts: 4.34 us -> 2.74 us
  Pallas kernels: 51.4 us -> 52.4 us
    unnamed x9 -> x1, local copies, waits for them, and re-layouts: 4.34 us -> 2.74 us
    pallas_call x1, Pallas kernels: 51.4 us -> 52.4 us  [local(): pl.pallas_call(kernel, out_shape=jax.ShapeDtypeStruct((16 * 6 * ROWS, LAN...]
where the time goes in v4:
time: 55.2 us; the launch traced here: 55.1 us
  Pallas kernels  52.4 us (95%)
  local copies, waits for them, and re-layouts  2.74 us (5%)
    pallas_call x1, Pallas kernels, local(): pl.pallas_call(kernel, out_shape=jax.ShapeDtypeStruct((16 * 6 * ROWS, LAN...  52.4 us
    unnamed x1, local copies, waits for them, and re-layouts  2.74 us

profile of v4, /device:TPU:1, one launch (start us, length us, event | category | flops | bytes accessed | tf_op | source)
XLA Modules:
  0.0 55.1 jit_solution(8166793292908982629)
XLA Ops:
  0.0 52.4 %adjoint.1 = f32[3072,128]{1,0:T(8,128)} custom-call(f32[1536,128]{1,0:T(8,128)} %bitcast.4, s32[16]{0:T(128)} %pos_hbm.1, s32[4,8,128]{2,1,0:T(8,128)} %bitcast.5, f32[8,8]{1,0:T(8,128)} %table_hbm.1), custom_call_target="tpu_custom_call" | custom-call | tf_op jit(solution)/shard_map/adjoint/pallas_call | solution.py:556
  52.4 2.7 %copy.6 = f32[16,2,3,32,128]{4,3,2,1,0:T(8,128)} copy(f32[16,2,3,32,128]{4,3,2,1,0:T(8,128)} %bitcast.3) | data formatting | bytes 3145728
